TPU v7x, 256 devices: a whole 4x4x8 slice. The times are simulated.
256 devices in a mesh: dp: 2 (over core), seq: 8 (over z), expert: 16 (over y, x).
Axes of the slice: x: 4, y: 4, z: 8, core: 2. Of those that a mesh axis runs over, the one named last changes fastest.
Arguments:
- tokens: bfloat16 [16384, 2048], P(('dp', 'seq')), may hold values from -6 to 6
- phi: bfloat16 [2048, 32], P(None, 'expert'), may hold values from -40 to 40
- w_in: bfloat16 [32, 2048, 8192], P('expert', None, ('dp', 'seq')), may hold values from -1 to 1
- w_out: bfloat16 [32, 8192, 2048], P('expert', ('dp', 'seq')), may hold values from -0.25 to 0.25
Outputs:
- mixed: bfloat16 [16384, 2048], P(('dp', 'seq', 'expert'))
All inputs are finite; a program needn't handle non-finite values.
Results may differ from a plain program's by a relative error of at most 0.0068.
Values may be sent and summed in bfloat16 or wider, within the bound.
A program may use at most 64 MiB of HBM per device.

v0:
```python
import jax
import jax.numpy as jnp
from jax import lax
from jax.sharding import PartitionSpec as P


def on_device(tokens, phi, w_in, w_out):
    n_expert = lax.axis_size("expert")
    rows_out = tokens.shape[0] // n_expert
    phi_all = lax.all_gather(phi, "expert", axis=1, tiled=True)
    logits = lax.dot_general(
        phi, tokens, (((0,), (1,)), ((), ())), preferred_element_type=jnp.float32
    )
    slot_max = lax.pmax(jnp.max(logits, axis=1), "seq")
    spread = jnp.exp(logits - slot_max[:, None])
    numerator = jnp.dot(spread.astype(jnp.bfloat16), tokens, preferred_element_type=jnp.float32)
    denominator = jnp.sum(spread, axis=1)
    numer_seq, denom_seq = lax.psum((numerator, denominator), "seq")
    own_slots = (numer_seq / denom_seq[:, None]).astype(jnp.bfloat16)
    slot_in = lax.all_gather(own_slots[None], "dp", axis=0, tiled=True)
    hidden = jax.nn.gelu(
        jnp.einsum("ced,edf->cef", slot_in, w_in, preferred_element_type=jnp.float32),
        approximate=True,
    ).astype(jnp.bfloat16)
    partial_value = jnp.einsum("cef,efd->ced", hidden, w_out, preferred_element_type=jnp.float32)
    totals = lax.psum(partial_value, ("dp", "seq"))
    summed = lax.dynamic_index_in_dim(totals, lax.axis_index("dp"), 0, keepdims=False)
    slot_out = lax.all_gather(summed.astype(jnp.bfloat16), "expert", axis=0, tiled=True)
    rows = lax.dynamic_slice_in_dim(tokens, lax.axis_index("expert") * rows_out, rows_out, 0)
    row_logits = lax.dot_general(
        phi_all, rows, (((0,), (1,)), ((), ())), preferred_element_type=jnp.float32
    )
    row_max = jnp.max(row_logits, axis=0)
    combine_weights = jnp.exp(row_logits - row_max[None, :])
    mixed_numer = lax.dot_general(
        combine_weights.astype(jnp.bfloat16),
        slot_out,
        (((0,), (0,)), ((), ())),
        preferred_element_type=jnp.float32,
    )
    mixed_denom = jnp.sum(combine_weights, axis=0)
    return (mixed_numer / mixed_denom[:, None]).astype(jnp.bfloat16)


def solution(mesh):
    placed = (
        P(("dp", "seq"), None),
        P(None, "expert"),
        P("expert", None, ("dp", "seq")),
        P("expert", ("dp", "seq"), None),
    )
    return jax.shard_map(
        on_device,
        mesh=mesh,
        in_specs=placed,
        out_specs=P(("dp", "seq", "expert"), None),
        check_vma=False,
    )
```

profile of v0, /device:TPU:32, one launch (start us, length us, event | category | flops | bytes accessed | tf_op | source)
XLA Modules:
  0.0 159.4 jit_solution(6288700102996713554)
XLA Ops:
  0.0 3.5 %fusion.39 = (f32[2]{0:T(128)S(1)}, f32[2,1024]{1,0:T(2,128)S(1)}) fusion(bf16[2048,2]{0,1:T(2,128)(2,1)} %param.5, bf16[1024,2048]{1,0:T(8,128)(2,1)} %param.4), kind=kOutput, calls=%fused_computation.39 | convolution fusion | flops 8390654 | bytes 4210696 | tf_op jit(solution)/shard_map/dot_general | solution.py:11
  3.5 17.9 %pmax.7 = f32[2]{0:T(128)S(1)} all-reduce(f32[2]{0:T(128)S(1)} %get-tuple-element.9), channel_id=1, replica_groups=mesh['dp'=2,'seq'=8,'expert'=16] {'seq'}, use_global_device_ids=true, to_apply=%region_2.0 | all-reduce | flops 2 | bytes 16 | tf_op jit(solution)/shard_map/pmax | solution.py:14
  21.4 0.2 fusion.25
  21.6 2.9 %fusion.27 = f32[2,2048]{1,0:T(2,128)S(1)} fusion(bf16[1024,2048]{1,0:T(8,128)(2,1)} %param.4, f32[2,1024]{1,0:T(2,128)S(1)} %get-tuple-element.10, f32[2]{0:T(128)S(1)} %pmax.7), kind=kOutput, calls=%fused_computation.28 | convolution fusion | flops 8392704 | bytes 4218888 | tf_op jit(solution)/shard_map/dot_general | solution.py:16
  24.5 27.9 %all-reduce = (f32[2,2048]{1,0:T(2,128)S(1)}, f32[2]{0:T(128)S(1)}) all-reduce(f32[2,2048]{1,0:T(2,128)S(1)} %fusion.27, f32[2]{0:T(128)S(1)} %fusion.25), channel_id=1, replica_groups=mesh['dp'=2,'seq'=8,'expert'=16] {'seq'}, use_global_device_ids=true, to_apply=%region_3.0 | all-reduce | flops 4098 | bytes 32784 | tf_op jit(solution)/shard_map/psum | solution.py:18
  52.4 0.1 fusion.24
  52.5 1.8 %all-gather.3 = bf16[2,2,2048]{2,1,0:T(2,128)(2,1)S(1)} all-gather(bf16[1,2,2048]{2,1,0:T(2,128)(2,1)S(1)} %fusion.24), channel_id=2, replica_groups=mesh['dp'=2,'seq'=8,'expert'=16] {'dp'}, dimensions={0}, use_global_device_ids=true | all-gather | bytes 24576 | tf_op jit(solution)/shard_map/all_gather | solution.py:20
  54.3 0.0 copy-start
  54.3 4.7 %convolution_bitcast_fusion = f32[2,2,2048]{2,0,1:T(2,128)S(1)} fusion(bf16[2,512,2048]{2,1,0:T(8,128)(2,1)} %param.7, bf16[2,2048,512]{2,1,0:T(8,128)(2,1)} %param.6, bf16[2,2,2048]{2,1,0:T(2,128)(2,1)S(1)} %all-gather.3), kind=kOutput, calls=%fused_computation.2 | convolution fusion | flops 16795648 | bytes 8437760 | tf_op jit(solution)/shard_map/cef,efd->ced/dot_general | solution.py:25
  59.0 51.1 %psum.23 = bf16[2,2,2048]{2,0,1:T(2,128)(2,1)S(1)} all-reduce(f32[2,2,2048]{2,0,1:T(2,128)S(1)} %convolution_bitcast_fusion), channel_id=1, replica_groups=mesh['dp'=2,'seq'=8,'expert'=16] {'dp','seq'}, use_global_device_ids=true, to_apply=%region_6.7 | all-reduce | flops 8192 | bytes 49152 | tf_op jit(solution)/shard_map/psum | solution.py:26
  110.1 0.0 copy-done
  110.1 24.0 %all-gather.2 = bf16[16,2,2048]{2,1,0:T(2,128)(2,1)S(1)} all-gather(bf16[1,2,2048]{2,1,0:T(2,128)(2,1)S(1)} %bitcast.24), channel_id=1, replica_groups=mesh['dp'=2,'seq'=8,'expert'=16] {'expert'}, dimensions={0}, use_global_device_ids=true | all-gather | bytes 139264 | tf_op jit(solution)/shard_map/all_gather | solution.py:10
  134.1 0.1 reshape.8
  134.1 1.2 fusion.38
  135.3 23.1 %all-gather.1 = bf16[1,32,2048]{2,0,1:T(2,128)(2,1)S(1)} all-gather(bf16[1,2,2048]{2,0,1:T(2,128)(2,1)S(1)} %dynamic-slice_convert_fusion), channel_id=3, replica_groups=mesh['dp'=2,'seq'=8,'expert'=16] {'expert'}, dimensions={1}, use_global_device_ids=true | all-gather | bytes 139264 | tf_op jit(solution)/shard_map/all_gather | solution.py:28
  158.4 1.0 fusion
  (2 shorter events, 0.1 us)
Async XLA Ops:
  54.3 55.8 %copy-start = (bf16[2048,2]{0,1:T(2,128)(2,1)S(1)}, bf16[2048,2]{0,1:T(2,128)(2,1)}, u32[]{:S(2)}) copy-start(bf16[2048,2]{0,1:T(2,128)(2,1)} %param.5) | copy-start | bytes 24580
where the time goes:
time: 160 us; the launch traced here: 159 us
  blocking collectives  146 us (91%)
  matrix products  13.2 us (8%)
    psum x1, blocking collectives, on_device(): totals = lax.psum(partial_value, ('dp', 'seq'))  51.1 us
    psum x1, blocking collectives, on_device(): numer_seq, denom_seq = lax.psum((numerator, denominator), 'seq')  27.9 us
    all_gather x1, blocking collectives, on_device(): phi_all = lax.all_gather(phi, 'expert', axis=1, tiled=True)  24 us
    all_gather x1, blocking collectives, on_device(): lax.all_gather(summed.astype(jnp.bfloat16), 'expert', axis=0, tiled=True)  23.1 us
    pmax x1, blocking collectives, on_device(): slot_max = lax.pmax(jnp.max(logits, axis=1), 'seq')  17.9 us
    dot_general x1, matrix products, on_device(): jnp.einsum('cef,efd->ced', hidden, w_out, preferred_element_type=jnp.floa...  4.66 us
    dot_general x1, matrix products, on_device(): lax.dot_general(phi, tokens, (((0,), (1,)), ((), ())), preferred_element_...  3.5 us

commit v1 on v0

--- a/solution.py
+++ b/solution.py
@@ -23,7 +23,7 @@
         approximate=True,
     ).astype(jnp.bfloat16)
     partial_value = jnp.einsum("cef,efd->ced", hidden, w_out, preferred_element_type=jnp.float32)
-    totals = lax.psum(partial_value, ("dp", "seq"))
+    totals = jnp.sum(lax.all_gather(partial_value, ("dp", "seq")), axis=0)
     summed = lax.dynamic_index_in_dim(totals, lax.axis_index("dp"), 0, keepdims=False)
     slot_out = lax.all_gather(summed.astype(jnp.bfloat16), "expert", axis=0, tiled=True)
     rows = lax.dynamic_slice_in_dim(tokens, lax.axis_index("expert") * rows_out, rows_out, 0)

time: 160 us -> 137 us (0.86)
  blocking collectives: 146 us -> 123 us
    psum x1 -> x0, blocking collectives: 51.1 us -> none  [on_device(): totals = lax.psum(partial_value, ('dp', 'seq'))]
    all_gather x0 -> x1, blocking collectives: none -> 28.5 us  [on_device(): totals = jnp.sum(lax.all_gather(partial_value, ('dp', 'seq')), axis=0)]
where the time goes in v1:
time: 137 us
  blocking collectives  123 us (90%)
  matrix products  13.2 us (10%)
    all_gather x1, blocking collectives, on_device(): totals = jnp.sum(lax.all_gather(partial_value, ('dp', 'seq')), axis=0)  28.5 us
    psum x1, blocking collectives, on_device(): numer_seq, denom_seq = lax.psum((numerator, denominator), 'seq')  28 us
    all_gather x1, blocking collectives, on_device(): lax.all_gather(summed.astype(jnp.bfloat16), 'expert', axis=0, tiled=True)  24 us
    all_gather x1, blocking collectives, on_device(): phi_all = lax.all_gather(phi, 'expert', axis=1, tiled=True)  23 us
    pmax x1, blocking collectives, on_device(): slot_max = lax.pmax(jnp.max(logits, axis=1), 'seq')  17.9 us
    dot_general x1, matrix products, on_device(): jnp.einsum('cef,efd->ced', hidden, w_out, preferred_element_type=jnp.floa...  4.66 us
    dot_general x1, matrix products, on_device(): lax.dot_general(phi, tokens, (((0,), (1,)), ((), ())), preferred_element_...  3.5 us
    dot_general x1, matrix products, on_device(): jnp.dot(spread.astype(jnp.bfloat16), tokens, preferred_element_type=jnp.f...  2.88 us

profile of v1, /device:TPU:32, one launch (start us, length us, event | category | flops | bytes accessed | tf_op | source)
XLA Modules:
  0.0 137.0 jit_solution(2608634129651959268)
XLA Ops:
  0.0 3.5 %fusion.39 = (f32[2]{0:T(128)S(1)}, f32[2,1024]{1,0:T(2,128)S(1)}) fusion(bf16[2048,2]{0,1:T(2,128)(2,1)} %param.5, bf16[1024,2048]{1,0:T(8,128)(2,1)} %param.4), kind=kOutput, calls=%fused_computation.40 | convolution fusion | flops 8390654 | bytes 4210696 | tf_op jit(solution)/shard_map/dot_general | solution.py:11
  3.5 17.9 %pmax.7 = f32[2]{0:T(128)S(1)} all-reduce(f32[2]{0:T(128)S(1)} %get-tuple-element.9), channel_id=1, replica_groups=mesh['dp'=2,'seq'=8,'expert'=16] {'seq'}, use_global_device_ids=true, to_apply=%region_2.0 | all-reduce | flops 2 | bytes 16 | tf_op jit(solution)/shard_map/pmax | solution.py:14
  21.4 2.9 %fusion.27 = f32[2,2048]{1,0:T(2,128)S(1)} fusion(bf16[1024,2048]{1,0:T(8,128)(2,1)} %param.4, f32[2,1024]{1,0:T(2,128)S(1)} %get-tuple-element.10, f32[2]{0:T(128)S(1)} %pmax.7), kind=kOutput, calls=%fused_computation.28 | convolution fusion | flops 8392704 | bytes 4218888 | tf_op jit(solution)/shard_map/dot_general | solution.py:16
  24.3 0.2 fusion.25
  24.5 28.0 %all-reduce = (f32[2,2048]{1,0:T(2,128)S(1)}, f32[2]{0:T(128)S(1)}) all-reduce(f32[2,2048]{1,0:T(2,128)S(1)} %fusion.27, f32[2]{0:T(128)S(1)} %fusion.25), channel_id=1, replica_groups=mesh['dp'=2,'seq'=8,'expert'=16] {'seq'}, use_global_device_ids=true, to_apply=%region_3.0 | all-reduce | flops 4098 | bytes 32784 | tf_op jit(solution)/shard_map/psum | solution.py:18
  52.4 0.1 fusion.24
  52.5 1.8 %all-gather.4 = bf16[2,2,2048]{2,1,0:T(2,128)(2,1)S(1)} all-gather(bf16[1,2,2048]{2,1,0:T(2,128)(2,1)S(1)} %fusion.24), channel_id=2, replica_groups=mesh['dp'=2,'seq'=8,'expert'=16] {'dp'}, dimensions={0}, use_global_device_ids=true | all-gather | bytes 24576 | tf_op jit(solution)/shard_map/all_gather | solution.py:20
  54.3 0.0 copy-start
  54.3 4.7 %convolution_bitcast_fusion = f32[2,2,2048]{2,0,1:T(2,128)S(1)} fusion(bf16[2,512,2048]{2,1,0:T(8,128)(2,1)} %param.7, bf16[2,2048,512]{2,1,0:T(8,128)(2,1)} %param.6, bf16[2,2,2048]{2,1,0:T(2,128)(2,1)S(1)} %all-gather.4), kind=kOutput, calls=%fused_computation.2 | convolution fusion | flops 16795648 | bytes 8437760 | tf_op jit(solution)/shard_map/cef,efd->ced/dot_general | solution.py:25
  59.0 28.5 %all-gather.1 = f32[32,2,2048]{2,1,0:T(2,128)S(1)} all-gather(f32[2,2,2048]{2,1,0:T(2,128)S(1)} %copy.10), channel_id=3, replica_groups=mesh['dp'=2,'seq'=8,'expert'=16] {'dp','seq'}, dimensions={0}, use_global_device_ids=true | all-gather | bytes 557056 | tf_op jit(solution)/shard_map/all_gather | solution.py:26
  87.5 0.2 reduce_sum.28
  87.7 24.0 %all-gather.2 = bf16[1,32,2048]{2,0,1:T(2,128)(2,1)S(1)} all-gather(bf16[1,2,2048]{2,0,1:T(2,128)(2,1)S(1)} %copy.28), channel_id=4, replica_groups=mesh['dp'=2,'seq'=8,'expert'=16] {'expert'}, dimensions={1}, use_global_device_ids=true | all-gather | bytes 139264 | tf_op jit(solution)/shard_map/all_gather | solution.py:28
  111.8 0.0 copy-done
  111.8 23.0 %all-gather.3 = bf16[16,2,2048]{2,1,0:T(2,128)(2,1)S(1)} all-gather(bf16[1,2,2048]{2,1,0:T(2,128)(2,1)S(1)} %bitcast.26), channel_id=1, replica_groups=mesh['dp'=2,'seq'=8,'expert'=16] {'expert'}, dimensions={0}, use_global_device_ids=true | all-gather | bytes 139264 | tf_op jit(solution)/shard_map/all_gather | solution.py:10
  134.8 0.1 reshape.9
  134.8 1.2 fusion.38
  136.0 1.0 fusion
  (4 shorter events, 0.1 us)
Async XLA Ops:
  54.3 57.5 %copy-start = (bf16[2048,2]{0,1:T(2,128)(2,1)S(1)}, bf16[2048,2]{0,1:T(2,128)(2,1)}, u32[]{:S(2)}) copy-start(bf16[2048,2]{0,1:T(2,128)(2,1)} %param.5) | copy-start | bytes 24580
